TPU v7x, 32 devices: a whole 2x2x4 slice. The times are simulated.
32 devices in a mesh: col: 16 (over z, x, core), row: 2 (over y).
Axes of the slice: x: 2, y: 2, z: 4, core: 2. Of those that a mesh axis runs over, the one named last changes fastest.
Arguments:
- uniq_rows: bfloat16 [32, 128, 1536], P('row', 'col'), may hold values from -6 to 6
- row_ids: int32 [32, 128, 8], P('row', 'col'), may hold values from 0 to 255, as said below
- sample_idx: int32 [512, 128], P('row', 'col'), may hold values from 0 to 7, as said below
- fm_proj: bfloat16 [128, 8], replicated, may hold values from -0.5 to 0.5
- ln_gain: float32 [1024], replicated, may hold values from 0.5 to 1.5
- w_up: bfloat16 [1024, 2048], P(None, 'row'), may hold values from -0.1875 to 0.1875
- w_down: bfloat16 [2048, 1536], P('row'), may hold values from -0.125 to 0.125
- w_lc: bfloat16 [8, 128], replicated, may hold values from -0.5 to 0.5
- w_res: bfloat16 [16, 128], replicated, may hold values from -0.5 to 0.5
- out_gain: float32 [192], replicated, may hold values from 0.5 to 1.5
- cotangent: bfloat16 [512, 3072], P(('row', 'col')), may hold values from -6 to 6
- moment1: float32 [128, 256, 192], P('col', 'row'), may hold values from -1.5 to 1.5
- moment2: float32 [128, 256], P('col', 'row'), may hold values from 0.01 to 0.1
Outputs:
- layer_out: bfloat16 [512, 3072], P(('row', 'col'))
- new_moment1: float32 [128, 256, 192], P('col', 'row')
- new_moment2: float32 [128, 256], P('col', 'row')
- row_step: float32 [128, 256, 192], P('col', 'row')
Inputs may be any that keep to these rules, and one draw needn't show every extreme that they name: `sample_idx`: for each block of 16 samples and each slot, every one of the 8 list entries is used by at least one sample of the block. `row_ids`: the 8 ids of one list are distinct. Row v of a slot is owned by index v // 128 of row. Of the 1024 list entries held by one device (the blocks of its index of row, the slots of its index of col), at most 640 name rows of one owner, and in every draw some owner is named exactly 640 times on each device.
All inputs are finite; a program needn't handle non-finite values.
Results may differ from a plain program's by a relative error of at most 0.005.
Values may be sent and summed in bfloat16 or wider, within the bound.
A program may use at most 64 MiB of HBM per device.

v0:
```python
import functools

import jax
import jax.numpy as jnp
from jax import lax
from jax.experimental import pallas as pl
from jax.experimental.pallas import tpu as pltpu
from jax.sharding import PartitionSpec as P

HIGH = lax.Precision.HIGHEST


def layer_norm(values, gain):
    centered = values - jnp.mean(values, -1, keepdims=True)
    inverse = lax.rsqrt(jnp.mean(centered * centered, -1, keepdims=True) + 1e-05)
    normed = centered * inverse
    return (normed * gain, normed, inverse)


def norm_back(grad_out, normed, inverse):
    first = jnp.mean(grad_out, -1, keepdims=True)
    second = jnp.mean(grad_out * normed, -1, keepdims=True)
    return (grad_out - first - normed * second) * inverse


def silu_grad(values):
    sigma = jax.nn.sigmoid(values)
    return sigma * (1.0 + values * (1.0 - sigma))


def plain_body(
    uniq_rows,
    row_ids,
    sample_idx,
    fm_proj,
    ln_gain,
    w_up,
    w_down,
    w_lc,
    w_res,
    out_gain,
    cotangent,
    moment1,
    moment2,
):
    columns = lax.axis_size("col")
    owners = lax.axis_size("row")
    slot_dev = uniq_rows.shape[1]
    width = out_gain.shape[0]
    uniq = uniq_rows.shape[2] // width
    samples = cotangent.shape[0]
    slots = slot_dev * columns
    vocab_dev = moment2.shape[1]
    rank = fm_proj.shape[1]
    fm_rows = w_down.shape[1] // width
    out_rows = w_res.shape[0]
    entry_iota = jnp.arange(uniq, dtype=jnp.int32)
    index_local = sample_idx.reshape(columns, samples, slot_dev)
    index = lax.all_to_all(index_local, "col", split_axis=0, concat_axis=2, tiled=True).reshape(
        samples, slots
    )
    picker = (index[:, :, None] == entry_iota).astype(jnp.bfloat16)
    moved = lax.all_to_all(uniq_rows, "col", split_axis=0, concat_axis=1, tiled=True)
    table = moved.reshape(slots, uniq, width)
    embed = jnp.einsum("stl,tle->ste", picker, table, preferred_element_type=jnp.float32).astype(
        jnp.bfloat16
    )
    compress = jnp.einsum("ste,tk->sek", embed, fm_proj, preferred_element_type=jnp.float32).astype(
        jnp.bfloat16
    )
    gram = jnp.einsum("ste,sek->stk", embed, compress, preferred_element_type=jnp.float32)
    flat = gram.reshape(samples, slots * rank)
    scaled, normed_in, inverse_in = layer_norm(flat, ln_gain)
    normal_in = scaled.astype(jnp.bfloat16)
    hidden_pre = jnp.dot(
        lax.all_gather(normal_in, "row", axis=0, tiled=True),
        w_up,
        preferred_element_type=jnp.float32,
    )
    hidden = jax.nn.silu(hidden_pre).astype(jnp.bfloat16)
    part_rows = hidden
    fm_out = lax.psum_scatter(
        jnp.dot(part_rows, w_down, preferred_element_type=jnp.float32),
        "row",
        scatter_dimension=0,
        tiled=True,
    )
    linear = jnp.einsum("lt,ste->sle", w_lc, embed, preferred_element_type=jnp.float32)
    joined = jnp.concatenate([fm_out.reshape(samples, fm_rows, width), linear], 1)
    normed_out, normed_rows, inverse_rows = layer_norm(joined, out_gain)
    residual = jnp.einsum("ot,ste->soe", w_res, embed, preferred_element_type=jnp.float32)
    layer_out = (normed_out + residual).reshape(samples, out_rows * width).astype(jnp.bfloat16)
    upstream = cotangent.astype(jnp.float32).reshape(samples, out_rows, width)
    grad_joined = norm_back(upstream * out_gain, normed_rows, inverse_rows)
    grad_fm = grad_joined[:, :fm_rows].reshape(samples, fm_rows * width).astype(jnp.bfloat16)
    grad_hidden = lax.dot_general(
        lax.all_gather(grad_fm, "row", axis=0, tiled=True),
        w_down,
        (((1,), (1,)), ((), ())),
        preferred_element_type=jnp.float32,
    )
    grad_pre = (grad_hidden * silu_grad(hidden_pre)).astype(jnp.bfloat16)
    part_rows = grad_pre
    grad_flat = lax.psum_scatter(
        lax.dot_general(
            part_rows, w_up, (((1,), (1,)), ((), ())), preferred_element_type=jnp.float32
        ).astype(jnp.bfloat16),
        "row",
        scatter_dimension=0,
        tiled=True,
    ).astype(jnp.float32)
    grad_gram = norm_back(grad_flat * ln_gain, normed_in, inverse_in).reshape(samples, slots, rank)
    grad_embed = jnp.einsum("stk,sek->ste", grad_gram, compress.astype(jnp.float32), precision=HIGH)
    grad_comp = jnp.einsum(
        "ste,stk->sek", embed, grad_gram, precision=HIGH, preferred_element_type=jnp.float32
    )
    grad_embed = grad_embed + jnp.einsum(
        "tk,sek->ste", fm_proj.astype(jnp.float32), grad_comp, precision=HIGH
    )
    grad_embed = grad_embed + jnp.einsum(
        "lt,sle->ste", w_lc.astype(jnp.float32), grad_joined[:, fm_rows:], precision=HIGH
    )
    grad_embed = grad_embed + jnp.einsum(
        "ot,soe->ste", w_res.astype(jnp.float32), upstream, precision=HIGH
    )
    list_grads = jnp.einsum("stl,ste->tle", picker.astype(jnp.float32), grad_embed, precision=HIGH)
    returned = lax.all_to_all(
        list_grads.reshape(columns, slot_dev, uniq * width),
        "col",
        split_axis=0,
        concat_axis=0,
        tiled=True,
    )
    entry_grads = returned.reshape(columns * slot_dev * uniq, width)
    row_list = row_ids.reshape(-1)
    slot_of = jnp.broadcast_to(
        jnp.arange(slot_dev, dtype=jnp.int32)[None, :, None], row_ids.shape
    ).reshape(-1)
    owner = row_list // vocab_dev
    target = slot_of * vocab_dev + row_list % vocab_dev
    span = slot_dev * vocab_dev
    entries = row_list.shape[0]
    capacity = 5 * entries // (4 * owners)
    onehot = (owner[:, None] == jnp.arange(owners, dtype=jnp.int32)).astype(jnp.int32)
    before = jnp.cumsum(onehot, 0) - onehot
    place = jnp.sum(before * onehot, 1)
    target_slot = owner * capacity + place
    bucket = jnp.zeros((owners * capacity, width), jnp.float32).at[target_slot].set(entry_grads)
    labels = (
        jnp.full((owners * capacity,), -1.0, jnp.float32)
        .at[target_slot]
        .set(target.astype(jnp.float32))
    )
    got_rows, got_labels = (
        lax.all_to_all(
            bucket.reshape(owners, capacity, width), "row", split_axis=0, concat_axis=0, tiled=True
        ),
        lax.all_to_all(
            labels.reshape(owners, capacity), "row", split_axis=0, concat_axis=0, tiled=True
        ),
    )
    segment = jnp.where(got_labels >= 0.0, got_labels, float(span)).astype(jnp.int32).reshape(-1)
    summed = jax.ops.segment_sum(got_rows.reshape(-1, width), segment, num_segments=span + 1)[:span]
    row_grads = summed.reshape(slot_dev, vocab_dev, width)
    new_moment1 = 0.9 * moment1 + 0.1 * row_grads
    new_moment2 = 0.99 * moment2 + 0.01 * jnp.mean(row_grads * row_grads, -1)
    row_step = new_moment1 * lax.rsqrt(new_moment2)[..., None]
    return (layer_out, new_moment1, new_moment2, row_step)


F32 = jnp.float32
BF16 = jnp.bfloat16
NT = (((1,), (1,)), ((), ()))


def iota(shape, dim):
    return lax.broadcasted_iota(jnp.int32, shape, dim)


def matmul(a, b, dims=(((1,), (0,)), ((), ())), precision=None):
    return lax.dot_general(a, b, dims, precision=precision, preferred_element_type=F32)


def fused_kernel(
    C,
    R,
    D,
    uniq,
    rid,
    sidx,
    fmp,
    gain,
    wup,
    wdn,
    wlc,
    wres,
    og,
    cot,
    lay_out,
    rg_out,
    isend,
    land,
    iland,
    wraw,
    wp,
    wd,
    t32,
    tst,
    lm,
    lmask,
    arep,
    rmat,
    nrm,
    ggr,
    idxn,
    nall,
    y,
    ds,
    fown,
    fsend,
    frecv,
    fm,
    gall,
    qown,
    qsend,
    qrecv,
    lay32,
    gf32,
    lg,
    sb,
    rland,
    oh,
    ps,
    pr,
    loc,
    s1,
    r1,
    si,
    ri,
    sa,
    ra,
    sbs,
    rbs,
    sc,
    rc,
    sx,
    rx,
):
    S, E, U, K, T = 16, 192, 8, 8, 128
    me = lax.axis_index("col")
    mr = lax.axis_index("row")

    def to_col(i):
        return lax.rem(me + i, C)

    def from_col(i):
        return lax.rem(me + C - i, C)

    def to_row(i):
        return lax.rem(mr + i, R)

    def from_row(i):
        return lax.rem(mr + R - i, R)

    def rcopy(src, dst, ssem, rsem, where):
        return pltpu.make_async_remote_copy(
            src_ref=src,
            dst_ref=dst,
            send_sem=ssem,
            recv_sem=rsem,
            device_id=where,
            device_id_type=pl.DeviceIdType.MESH,
        )

    cp_up = pltpu.make_async_copy(wup, wraw, loc.at[0])
    cp_dn = pltpu.make_async_copy(wdn, wd, loc.at[1])
    own_rows = pltpu.make_async_copy(uniq.at[me], land.at[me], loc.at[2])
    own_rows.start()

    barrier = pltpu.get_barrier_semaphore()
    for i in range(1, C):
        pl.semaphore_signal(
            barrier, inc=1, device_id={"col": to_col(i)}, device_id_type=pl.DeviceIdType.MESH
        )
    for i in range(1, R):
        pl.semaphore_signal(
            barrier, inc=1, device_id={"row": to_row(i)}, device_id_type=pl.DeviceIdType.MESH
        )
    for p in range(C):
        at = p * S % T
        tile = sidx[:, p * S // T * T : (p * S // T + 1) * T]
        if at:
            tile = pltpu.roll(tile, T - at, 1)
        isend[p] = tile[:, :S]
    iland[me] = isend[me]
    pl.semaphore_wait(barrier, C + R - 2)

    order = sorted(range(1, C), key=lambda i: -min(i, C - i))
    idx_copies, row_copies = [], []
    for i in order:
        p = to_col(i)
        idx_copies.append(rcopy(isend.at[p], iland.at[me], si.at[i], ri.at[i], {"col": p}))
        idx_copies[-1].start()
    for i in order:
        p = to_col(i)
        row_copies.append(rcopy(uniq.at[p], land.at[me], s1.at[i], r1.at[i], {"col": p}))
        row_copies[-1].start()

    cp_up.start()
    cp_dn.start()

    to, at = iota((256, 256), 0), iota((256, 256), 1)
    perm = (((to & 31) * 8 + (to >> 5)) == at).astype(F32).astype(BF16)
    cp_up.wait()
    for g in range(4):
        blk = matmul(perm, wraw[g * 256 : (g + 1) * 256, :]).astype(BF16)
        for k in range(K):
            wp[k * T + g * 32 : k * T + (g + 1) * 32, :] = blk[k * 32 : (k + 1) * 32, :]
    lane = iota((K, K * T), 1)
    spread = jnp.where((lane & 7) == iota((K, K * T), 0), gain[...], 0.0)
    fold = ((iota((K * T, T), 0) >> 3) == iota((K * T, T), 1)).astype(F32)
    gk = matmul(spread, fold, precision=HIGH)

    amat = jnp.concatenate(
        [
            fmp[...].astype(F32),
            wlc[...].astype(F32),
            wres[...].astype(F32),
        ],
        0,
    )
    for j in range(32):
        arep[j * S : (j + 1) * S, :] = jnp.broadcast_to(amat[j : j + 1, :], (S, T))

    place = (iota((C, T), 0) == (iota((C, T), 1) >> 3)).astype(F32)
    wide = matmul(rid[...].astype(F32).reshape(D * U, C), place, precision=HIGH).reshape(D, U, T)
    mine = iota((D, U, T), 1) == (iota((D, U, T), 2) & (U - 1))
    labels = jnp.sum(jnp.where(mine, wide, 0.0), 1).astype(jnp.int32)
    target = iota((T, T), 0)
    for i in range(R):
        local = labels - to_row(i) * T
        for d in range(D):
            oh[i, d] = jnp.where(
                target == jnp.broadcast_to(local[d : d + 1, :], (T, T)), 1.0, 0.0
            ).astype(BF16)

    for cp in idx_copies:
        cp.wait_recv()
    ix = iland[...].astype(F32).reshape(T, S)
    tiled = (iota((S, T), 0) == (iota((S, T), 1) & (S - 1))).astype(F32)
    idx_n = matmul(ix, tiled, precision=HIGH)
    idxn[...] = idx_n
    idx_t = idx_n.T
    for u in range(U):
        for q in range(4):
            lm[q * T : (q + 1) * T, u * T : (u + 1) * T] = jnp.where(
                idx_t == float(u), arep[q * T : (q + 1) * T, :], 0.0
            ).astype(BF16)
    entry = iota((U, T), 0).astype(F32)

    def fill(src, q):
        for t in range(0, T, 2):
            rows = [
                jnp.where(
                    jnp.broadcast_to(idxn[v : v + 1, :], (U, T)) == entry,
                    jnp.broadcast_to(src[v : v + 1, :], (U, T)),
                    0.0,
                )
                for v in (t, t + 1)
            ]
            lmask[t * U : (t + 2) * U, q * T : (q + 1) * T] = jnp.concatenate(rows, 0).astype(BF16)

    for q in range(4):
        ggr[...] = arep[q * T : (q + 1) * T, :].T
        fill(ggr, q)
    upstream = cot[...].astype(F32)
    for o in range(16):
        rmat[(16 + o) * S : (17 + o) * S, :] = upstream[:, o * E : (o + 1) * E].astype(BF16)

    own_rows.wait()
    for cp in row_copies:
        cp.wait_recv()
    t32[...] = land[...].astype(F32).reshape(T, U * E)
    for u in range(U):
        tst[u * T : (u + 1) * T, :] = t32[:, u * E : (u + 1) * E].astype(BF16)

    comp = matmul(lm[0:T, :], tst[...]).astype(BF16)
    rmat[512:640, :] = comp
    z = matmul(comp, tst[...], NT)
    gram = jnp.where(idx_t == 0.0, z[:, 0:T], 0.0)
    for u in range(1, U):
        gram = gram + jnp.where(idx_t == float(u), z[:, u * T : (u + 1) * T], 0.0)
    n_flat = float(K * T)
    g3 = gram.reshape(K, S, T)
    mu = jnp.sum(jnp.sum(g3, 0), -1, keepdims=True) / n_flat
    cent = g3 - mu[None]
    inv_in = lax.rsqrt(jnp.sum(jnp.sum(cent * cent, 0), -1, keepdims=True) / n_flat + 1e-05)
    normed_in = cent * inv_in[None]
    nrm[...] = normed_in.reshape(K * S, T)
    for k in range(K):
        nall[mr, :, k * T : (k + 1) * T] = (normed_in[k] * gk[k : k + 1, :]).astype(BF16)

    def row_send(stage, src_of, dst):
        copies = []
        for i in range(1, R):
            p = to_row(i)
            sem = stage * R + i
            copies.append(rcopy(src_of(p), dst.at[mr], sx.at[sem], rx.at[sem], {"row": p}))
            copies[-1].start()
        return copies

    n_copies = row_send(0, lambda p: nall.at[mr], nall)
    y[...] = matmul(lm[T:512, :], tst[...])
    cp_dn.wait()
    for cp in n_copies:
        cp.wait_recv()
    hp = matmul(nall[...].reshape(R * S, K * T), wp[...])
    sg = jax.nn.sigmoid(hp)
    hid = (hp * sg).astype(BF16)
    fp = matmul(hid, wd[...]).reshape(R, S, 8 * E)
    fsend[...] = fp.astype(BF16)
    fown[...] = fp
    f_copies = row_send(1, lambda p: fsend.at[p], frecv)
    ds[...] = sg * (1.0 + hp * (1.0 - sg))

    gain_out = og[...]
    up_fm = jnp.concatenate([upstream[:, o * E : (o + 1) * E] for o in range(8)], 0) * gain_out
    up_mean = jnp.mean(up_fm, -1, keepdims=True)

    def out_norm(joined, o):
        up = upstream[:, o * E : (o + 1) * E]
        c = joined - jnp.mean(joined, -1, keepdims=True)
        inv = lax.rsqrt(jnp.mean(c * c, -1, keepdims=True) + 1e-05)
        nr = c * inv
        return nr, norm_back(up * gain_out, nr, inv)

    for o in range(8, 16):
        nr, gj = out_norm(y[(o - 8) * S : (o - 7) * S, :], o)
        lay32[:, o * E : (o + 1) * E] = nr * gain_out + y[(8 + o) * S : (9 + o) * S, :]
        rmat[o * S : (o + 1) * S, :] = gj.astype(BF16)

    for cp in f_copies:
        cp.wait_recv()
    total = fown[mr]
    for i in range(1, R):
        total = total + frecv[from_row(i)].astype(F32)
    fm[...] = total
    joined = jnp.concatenate([fm[:, o * E : (o + 1) * E] for o in range(8)], 0)
    cen = joined - jnp.mean(joined, -1, keepdims=True)
    inv_fm = lax.rsqrt(jnp.mean(cen * cen, -1, keepdims=True) + 1e-05)
    normed_fm = cen * inv_fm
    across = jnp.mean(up_fm * cen, -1, keepdims=True) * inv_fm
    grad_fm = (up_fm - up_mean - normed_fm * across) * inv_fm
    for o in range(8):
        gf32[:, o * E : (o + 1) * E] = grad_fm[o * S : (o + 1) * S]
    gall[mr] = gf32[...].astype(BF16)
    g_copies = row_send(2, lambda p: gall.at[mr], gall)
    for o in range(8):
        lay32[:, o * E : (o + 1) * E] = (
            normed_fm[o * S : (o + 1) * S] * gain_out + y[(8 + o) * S : (9 + o) * S, :]
        )
    lay_out[...] = lay32[...].astype(BF16)
    for cp in g_copies:
        cp.wait_recv()
    gh = matmul(gall[...].reshape(R * S, 8 * E), wd[...], NT)
    gp = (gh * ds[...]).astype(BF16)
    gq = matmul(gp, wp[...], NT).reshape(R, S, K * T)
    qsend[...] = gq.astype(BF16)
    qown[...] = gq
    q_copies = row_send(3, lambda p: qsend.at[p], qrecv)
    for cp in q_copies:
        cp.wait_recv()
    gflat = qown[mr]
    for i in range(1, R):
        gflat = gflat + qrecv[from_row(i)].astype(F32)
    qs = [gflat[:, k * T : (k + 1) * T] * gk[k : k + 1, :] for k in range(K)]
    ns = [nrm[k * S : (k + 1) * S, :] for k in range(K)]
    first = jnp.sum(sum(qs), -1, keepdims=True) / n_flat
    second = jnp.sum(sum(q * n for q, n in zip(qs, ns)), -1, keepdims=True) / n_flat
    for k in range(K):
        ggr[k * S : (k + 1) * S, :] = (qs[k] - first - ns[k] * second) * inv_in
    gg = ggr[...]
    for u in range(U):
        lm[0:T, u * T : (u + 1) * T] = jnp.where(idx_t == float(u), gg, 0.0).astype(BF16)
    ggr[...] = gg.T
    fill(ggr, 4)
    rmat[0:T, :] = matmul(lm[0:T, :], tst[...]).astype(BF16)
    lg[...] = matmul(lmask[...], rmat[...])

    top = lg[:, T:E].reshape(C, D * U, E - T)
    sb[:, 64:96, :] = jnp.concatenate([top[:, :32], top[:, 32:]], -1).astype(BF16)
    sb[:, 0:64, :] = lg[:, 0:T].reshape(C, D * U, T).astype(BF16)
    cuts = (pl.ds(64, 32), pl.ds(0, 32), pl.ds(32, 32))
    sems = ((sbs, rbs), (sa, ra), (sc, rc))
    g_in = []

    def send_lists(stage):
        cut, (ssem, rsem) = cuts[stage], sems[stage]
        g_in.append([])
        for i in order:
            p = to_col(i)
            g_in[stage].append(
                rcopy(sb.at[p, cut], rland.at[me, cut], ssem.at[i], rsem.at[i], {"col": p})
            )
            g_in[stage][-1].start()

    send_lists(0)
    send_lists(1)
    rland[me] = sb[me]

    p_copies = []
    for stage in range(3):
        for cp in g_in[stage]:
            cp.wait_recv()
        pieces = []
        for p in range(2):
            start = (64, 0, 32)[stage] + p * 16
            both = rland[:, start : start + 16, :].astype(F32)
            for h in range(2):
                x = both[:, h * U : (h + 1) * U, :].reshape(T, T).T.astype(BF16)
                d = 2 * p + h
                if stage == 0:
                    pieces.append((d, T, E, x[: E - T]))
                    pieces.append((d + 4, T, E, x[E - T :]))
                else:
                    pieces.append((d + 4 * (stage - 1), 0, T, x))
        for i in range(1, R):
            for d, a, b, x in pieces:
                ps[i, d, a:b, :] = matmul(x, oh[i, d], NT).astype(BF16)
            part = (slice(0, D), slice(T, E)) if stage == 0 else (
                slice(4 * (stage - 1), 4 * stage),
                slice(0, T),
            )
            ds_of = tuple(pl.ds(q.start, q.stop - q.start) for q in part)
            sem = (4 + stage) * R + i
            p_copies.append(
                rcopy(
                    ps.at[(i,) + ds_of],
                    pr.at[(i,) + ds_of],
                    sx.at[sem],
                    rx.at[sem],
                    {"row": to_row(i)},
                )
            )
            p_copies[-1].start()
        if stage == 0:
            send_lists(2)
        for d, a, b, x in pieces:
            rg_out[d, a:b, :] = matmul(x, oh[0, d], NT)
    for cp in p_copies:
        cp.wait_recv()
    for i in range(1, R):
        rg_out[...] += pr[i].astype(F32)

    for group in (
        idx_copies,
        row_copies,
        n_copies,
        f_copies,
        g_copies,
        q_copies,
        g_in[0],
        g_in[1],
        g_in[2],
        p_copies,
    ):
        for cp in group:
            cp.wait_send()


def moment_kernel(width, lay, grads, m1, m2, lay_out, m1_out, m2_out, step_out):
    lay_out[...] = lay[...]
    for h in range(4):
        row = pl.ds(pl.program_id(0) * 4 + h, 1)
        g = grads[h]
        first = 0.9 * m1[h] + 0.1 * g
        second = 0.99 * m2[row, :] + 0.01 * (jnp.sum(g * g, 0, keepdims=True) / width)
        m1_out[h] = first
        m2_out[row, :] = second
        step_out[h] = first * lax.rsqrt(second)


def fast_body(
    C,
    R,
    uniq_rows,
    row_ids,
    sample_idx,
    fm_proj,
    ln_gain,
    w_up,
    w_down,
    w_lc,
    w_res,
    out_gain,
    cotangent,
    moment1,
    moment2,
):
    D = uniq_rows.shape[1]
    S = cotangent.shape[0]
    hid = w_up.shape[1]
    wide = w_down.shape[1]
    flat = w_up.shape[0]
    width = out_gain.shape[0]
    T = C * D
    vmem = pl.BlockSpec(memory_space=pltpu.VMEM)
    hbm = pl.BlockSpec(memory_space=pl.ANY)
    dma = pltpu.SemaphoreType.DMA
    layer_out, row_grads = pl.pallas_call(
        functools.partial(fused_kernel, C, R, D),
        out_shape=(
            jax.ShapeDtypeStruct((S, 16 * width), BF16),
            jax.ShapeDtypeStruct((D, width, T), F32),
        ),
        in_specs=[hbm, vmem, vmem, vmem, vmem, hbm, hbm, vmem, vmem, vmem, vmem],
        out_specs=(vmem, vmem),
        scratch_shapes=[
            pltpu.VMEM((C, D, S), jnp.int32),
            pltpu.VMEM((C, D, wide), BF16),
            pltpu.VMEM((C, D, S), jnp.int32),
            pltpu.VMEM((flat, hid), BF16),
            pltpu.VMEM((flat, hid), BF16),
            pltpu.VMEM((hid, wide), BF16),
            pltpu.VMEM((T, wide), F32),
            pltpu.VMEM((8 * T, width), BF16),
            pltpu.VMEM((512, 8 * T), BF16),
            pltpu.VMEM((8 * T, 640), BF16),
            pltpu.VMEM((512, T), F32),
            pltpu.VMEM((640, width), BF16),
            pltpu.VMEM((128, T), F32),
            pltpu.VMEM((128, T), F32),
            pltpu.VMEM((T, 128), F32),
            pltpu.VMEM((R, S, flat), BF16),
            pltpu.VMEM((384, width), F32),
            pltpu.VMEM((R * S, hid), F32),
            pltpu.VMEM((R, S, wide), F32),
            pltpu.VMEM((R, S, wide), BF16),
            pltpu.VMEM((R, S, wide), BF16),
            pltpu.VMEM((S, wide), F32),
            pltpu.VMEM((R, S, wide), BF16),
            pltpu.VMEM((R, S, flat), F32),
            pltpu.VMEM((R, S, flat), BF16),
            pltpu.VMEM((R, S, flat), BF16),
            pltpu.VMEM((S, 16 * width), F32),
            pltpu.VMEM((S, wide), F32),
            pltpu.VMEM((8 * T, width), F32),
            pltpu.VMEM((C, 12 * D, T), BF16),
            pltpu.VMEM((C, 12 * D, T), BF16),
            pltpu.VMEM((R, D, T, T), BF16),
            pltpu.VMEM((R, D, width, T), BF16),
            pltpu.VMEM((R, D, width, T), BF16),
            dma((4,)),
            dma((C,)),
            dma((C,)),
            dma((C,)),
            dma((C,)),
            dma((C,)),
            dma((C,)),
            dma((C,)),
            dma((C,)),
            dma((C,)),
            dma((C,)),
            dma((7 * R,)),
            dma((7 * R,)),
        ],
        compiler_params=pltpu.CompilerParams(
            collective_id=0, has_side_effects=True, vmem_limit_bytes=56 * 1024 * 1024
        ),
        name="wukong_step",
    )(
        uniq_rows,
        row_ids.transpose(1, 2, 0),
        sample_idx.T,
        fm_proj.T,
        ln_gain.reshape(1, flat),
        w_up,
        w_down,
        w_lc,
        w_res,
        out_gain.reshape(1, width),
        cotangent,
    )
    slab = pl.BlockSpec((4, width, T), lambda d: (d, 0, 0))
    whole = pl.BlockSpec((D, T), lambda d: (0, 0))
    strip = pl.BlockSpec((S, 8 * width), lambda d: (0, d))
    layer_out, new_moment1, new_moment2, row_step = pl.pallas_call(
        functools.partial(moment_kernel, width),
        grid=(D // 4,),
        out_shape=(
            jax.ShapeDtypeStruct((S, 16 * width), BF16),
            jax.ShapeDtypeStruct((D, width, T), F32),
            jax.ShapeDtypeStruct((D, T), F32),
            jax.ShapeDtypeStruct((D, width, T), F32),
        ),
        in_specs=[strip, slab, slab, whole],
        out_specs=(strip, slab, whole, slab),
        name="moments",
    )(layer_out, row_grads, moment1.transpose(0, 2, 1), moment2)
    return (
        layer_out,
        new_moment1.transpose(0, 2, 1),
        new_moment2,
        row_step.transpose(0, 2, 1),
    )


def step(C, R, *args):
    if args[0].shape[1] == 8 and C == 16:
        return fast_body(C, R, *args)
    return plain_body(*args)


def solution(mesh):
    return jax.shard_map(
        functools.partial(step, mesh.shape["col"], mesh.shape["row"]),
        mesh=mesh,
        in_specs=(
            P("row", "col", None),
            P("row", "col", None),
            P("row", "col"),
            P(),
            P(),
            P(None, "row"),
            P("row", None),
            P(),
            P(),
            P(),
            P(("row", "col"), None),
            P("col", "row", None),
            P("col", "row"),
        ),
        out_specs=(
            P(("row", "col"), None),
            P("col", "row", None),
            P("col", "row"),
            P("col", "row", None),
        ),
        check_vma=False,
    )
```

profile of v0, /device:TPU:0, one launch (start us, length us, event | category | flops | bytes accessed | tf_op | source)
XLA Modules:
  0.0 57.5 jit_solution(2942115318562266016)
XLA Ops:
  0.6 54.4 %wukong_step.1 = (bf16[16,3072]{1,0:T(8,128)(2,1)}, f32[8,192,128]{2,1,0:T(8,128)}) custom-call(bf16[16,8,1536]{2,1,0:T(8,128)(2,1)} %uniq.1, s32[8,8,16]{2,1,0:T(8,128)} %bitcast.9, s32[8,256]{1,0:T(8,128)} %bitcast.10, bf16[8,128]{1,0:T(8,128)(2,1)} %bitcast.12, f32[1,1024]{1,0:T(1,128)} %bitcast.11, bf16[1024,1024]{1,0:T(8,128)(2,1)} %wup.1, ...), custom_call_target="tpu_custom_call" | custom-call | tf_op jit(solution)/shard_map/wukong_step/pallas_call | solution.py:610
  55.1 2.4 %moments.1 = (bf16[16,3072]{1,0:T(8,128)(2,1)}, f32[8,192,128]{2,1,0:T(8,128)}, f32[8,128]{1,0:T(8,128)}, f32[8,192,128]{2,1,0:T(8,128)}) custom-call(bf16[16,3072]{1,0:T(8,128)(2,1)} %get-tuple-element.10.lay, f32[8,192,128]{2,1,0:T(8,128)} %get-tuple-element.11.grads, f32[8,192,128]{2,1,0:T(8,128)} %bitcast.8, f32[8,128]{1,0:T(8,128)} %m2.1), custom_call_target="tpu_custom_call" | custom-call | tf_op jit(solution)/shard_map/moments/pallas_call | solution.py:687
where the time goes:
time: 57.7 us; the launch traced here: 57.5 us
  Pallas kernels  56.8 us (98%)
  between operations  0.64 us (1%)
    pallas_call x1, Pallas kernels, fast_body(): pl.pallas_call(functools.partial(fused_kernel, C, R, D), out_shape=(jax.S...  54.4 us
    pallas_call x1, Pallas kernels, fast_body(): pl.pallas_call(functools.partial(moment_kernel, width), grid=(D // 4,), o...  2.39 us

commit v1 on v0

--- a/solution.py
+++ b/solution.py
@@ -183,21 +183,34 @@
 
 def fused_kernel(
     C,
-    R,
     D,
     uniq,
+    rid_in,
+    sidx_in,
+    fmp_in,
+    gain_in,
+    wup,
+    wdn,
+    wlc_in,
+    wres_in,
+    og_in,
+    cot_in,
+    m1_in,
+    m2_in,
+    lay_out,
+    rg_out,
+    pr,
+    m1_out,
+    m2_out,
     rid,
     sidx,
     fmp,
     gain,
-    wup,
-    wdn,
     wlc,
     wres,
     og,
     cot,
-    lay_out,
-    rg_out,
+    cpeer,
     isend,
     land,
     iland,
@@ -216,51 +229,38 @@
     nall,
     y,
     ds,
-    fown,
+    c32,
     fsend,
     frecv,
     fm,
-    gall,
-    qown,
     qsend,
     qrecv,
+    gq,
     lay32,
     gf32,
-    lg,
+    lge,
     sb,
     rland,
     oh,
     ps,
-    pr,
     loc,
     s1,
     r1,
     si,
     ri,
-    sa,
-    ra,
-    sbs,
-    rbs,
-    sc,
-    rc,
+    su,
+    ru,
     sx,
     rx,
 ):
     S, E, U, K, T = 16, 192, 8, 8, 128
+    FC, QC = 3, 2
     me = lax.axis_index("col")
     mr = lax.axis_index("row")
+    other = 1 - mr
 
     def to_col(i):
         return lax.rem(me + i, C)
-
-    def from_col(i):
-        return lax.rem(me + C - i, C)
-
-    def to_row(i):
-        return lax.rem(mr + i, R)
-
-    def from_row(i):
-        return lax.rem(mr + R - i, R)
 
     def rcopy(src, dst, ssem, rsem, where):
         return pltpu.make_async_remote_copy(
@@ -272,20 +272,47 @@
             device_id_type=pl.DeviceIdType.MESH,
         )
 
-    cp_up = pltpu.make_async_copy(wup, wraw, loc.at[0])
-    cp_dn = pltpu.make_async_copy(wdn, wd, loc.at[1])
-    own_rows = pltpu.make_async_copy(uniq.at[me], land.at[me], loc.at[2])
-    own_rows.start()
+    def row_send(src, dst, sem):
+        copy = rcopy(src, dst, sx.at[sem], rx.at[sem], {"row": other})
+        copy.start()
+        return copy
 
     barrier = pltpu.get_barrier_semaphore()
     for i in range(1, C):
         pl.semaphore_signal(
             barrier, inc=1, device_id={"col": to_col(i)}, device_id_type=pl.DeviceIdType.MESH
         )
-    for i in range(1, R):
-        pl.semaphore_signal(
-            barrier, inc=1, device_id={"row": to_row(i)}, device_id_type=pl.DeviceIdType.MESH
+    pl.semaphore_signal(
+        barrier, inc=1, device_id={"row": other}, device_id_type=pl.DeviceIdType.MESH
+    )
+    cp_idx = pltpu.make_async_copy(sidx_in, sidx, loc.at[0])
+    cp_idx.start()
+    cp_up = pltpu.make_async_copy(wup, wraw, loc.at[1])
+    cp_dn = pltpu.make_async_copy(wdn, wd, loc.at[2])
+    own_rows = pltpu.make_async_copy(uniq.at[me], land.at[me], loc.at[3])
+    own_rows.start()
+    small = [
+        pltpu.make_async_copy(a, b, loc.at[4 + n])
+        for n, (a, b) in enumerate(
+            (
+                (rid_in, rid),
+                (fmp_in, fmp),
+                (gain_in, gain),
+                (wlc_in, wlc),
+                (wres_in, wres),
+                (og_in, og),
+                (cot_in, cot),
+                (m2_in, m2_out),
+            )
         )
+    ]
+    for cp in small:
+        cp.start()
+    cp_m1 = pltpu.make_async_copy(m1_in, m1_out, loc.at[12])
+    cp_up.start()
+    cp_dn.start()
+    cp_m1.start()
+    cp_idx.wait()
     for p in range(C):
         at = p * S % T
         tile = sidx[:, p * S // T * T : (p * S // T + 1) * T]
@@ -293,7 +320,7 @@
             tile = pltpu.roll(tile, T - at, 1)
         isend[p] = tile[:, :S]
     iland[me] = isend[me]
-    pl.semaphore_wait(barrier, C + R - 2)
+    pl.semaphore_wait(barrier, C)
 
     order = sorted(range(1, C), key=lambda i: -min(i, C - i))
     idx_copies, row_copies = [], []
@@ -305,12 +332,12 @@
         p = to_col(i)
         row_copies.append(rcopy(uniq.at[p], land.at[me], s1.at[i], r1.at[i], {"col": p}))
         row_copies[-1].start()
-
-    cp_up.start()
-    cp_dn.start()
+    c_copy = row_send(cot_in.at[:, pl.ds(0, 8 * E)], cpeer, 0)
 
     to, at = iota((256, 256), 0), iota((256, 256), 1)
     perm = (((to & 31) * 8 + (to >> 5)) == at).astype(F32).astype(BF16)
+    for cp in small:
+        cp.wait()
     cp_up.wait()
     for g in range(4):
         blk = matmul(perm, wraw[g * 256 : (g + 1) * 256, :]).astype(BF16)
@@ -337,8 +364,8 @@
     mine = iota((D, U, T), 1) == (iota((D, U, T), 2) & (U - 1))
     labels = jnp.sum(jnp.where(mine, wide, 0.0), 1).astype(jnp.int32)
     target = iota((T, T), 0)
-    for i in range(R):
-        local = labels - to_row(i) * T
+    for i in range(2):
+        local = labels - (mr if i == 0 else other) * T
         for d in range(D):
             oh[i, d] = jnp.where(
                 target == jnp.broadcast_to(local[d : d + 1, :], (T, T)), 1.0, 0.0
@@ -358,7 +385,7 @@
             ).astype(BF16)
     entry = iota((U, T), 0).astype(F32)
 
-    def fill(src, q):
+    def fill(src, at):
         for t in range(0, T, 2):
             rows = [
                 jnp.where(
@@ -368,14 +395,16 @@
                 )
                 for v in (t, t + 1)
             ]
-            lmask[t * U : (t + 2) * U, q * T : (q + 1) * T] = jnp.concatenate(rows, 0).astype(BF16)
+            lmask[t // D, t % D * U : (t % D + 2) * U, at * T : (at + 1) * T] = jnp.concatenate(
+                rows, 0
+            ).astype(BF16)
 
     for q in range(4):
         ggr[...] = arep[q * T : (q + 1) * T, :].T
-        fill(ggr, q)
+        fill(ggr, (q + 3) & 3)
     upstream = cot[...].astype(F32)
     for o in range(16):
-        rmat[(16 + o) * S : (17 + o) * S, :] = upstream[:, o * E : (o + 1) * E].astype(BF16)
+        rmat[(8 + o) * S : (9 + o) * S, :] = upstream[:, o * E : (o + 1) * E].astype(BF16)
 
     own_rows.wait()
     for cp in row_copies:
@@ -398,34 +427,30 @@
     normed_in = cent * inv_in[None]
     nrm[...] = normed_in.reshape(K * S, T)
     for k in range(K):
-        nall[mr, :, k * T : (k + 1) * T] = (normed_in[k] * gk[k : k + 1, :]).astype(BF16)
-
-    def row_send(stage, src_of, dst):
-        copies = []
-        for i in range(1, R):
-            p = to_row(i)
-            sem = stage * R + i
-            copies.append(rcopy(src_of(p), dst.at[mr], sx.at[sem], rx.at[sem], {"row": p}))
-            copies[-1].start()
-        return copies
-
-    n_copies = row_send(0, lambda p: nall.at[mr], nall)
+        nall[0, :, k * T : (k + 1) * T] = (normed_in[k] * gk[k : k + 1, :]).astype(BF16)
+    n_copy = row_send(nall.at[0], nall.at[1], 1)
+
     y[...] = matmul(lm[T:512, :], tst[...])
+    gain_out = og[...]
+    c_copy.wait_recv()
+    c32[0:S, :] = upstream[:, 0 : 8 * E]
+    c32[S : 2 * S, :] = cpeer[...].astype(F32)
+    up_fm = jnp.concatenate([c32[:, o * E : (o + 1) * E] for o in range(8)], 0) * gain_out
+    up_mean = jnp.mean(up_fm, -1, keepdims=True)
     cp_dn.wait()
-    for cp in n_copies:
-        cp.wait_recv()
-    hp = matmul(nall[...].reshape(R * S, K * T), wp[...])
+    n_copy.wait_recv()
+    hp = matmul(nall[...].reshape(2 * S, K * T), wp[...])
     sg = jax.nn.sigmoid(hp)
     hid = (hp * sg).astype(BF16)
-    fp = matmul(hid, wd[...]).reshape(R, S, 8 * E)
-    fsend[...] = fp.astype(BF16)
-    fown[...] = fp
-    f_copies = row_send(1, lambda p: fsend.at[p], frecv)
+    f_copies = []
+    for c in range(FC):
+        cols = slice(c * 8 * E // FC, (c + 1) * 8 * E // FC)
+        fp = matmul(hid, wd[:, cols])
+        fm[:, cols] = fp
+        fsend[c, 0:S] = fp[S : 2 * S].astype(BF16)
+        fsend[c, S : 2 * S] = fp[0:S].astype(BF16)
+        f_copies.append(row_send(fsend.at[c], frecv.at[c], 2 + c))
     ds[...] = sg * (1.0 + hp * (1.0 - sg))
-
-    gain_out = og[...]
-    up_fm = jnp.concatenate([upstream[:, o * E : (o + 1) * E] for o in range(8)], 0) * gain_out
-    up_mean = jnp.mean(up_fm, -1, keepdims=True)
 
     def out_norm(joined, o):
         up = upstream[:, o * E : (o + 1) * E]
@@ -437,14 +462,12 @@
     for o in range(8, 16):
         nr, gj = out_norm(y[(o - 8) * S : (o - 7) * S, :], o)
         lay32[:, o * E : (o + 1) * E] = nr * gain_out + y[(8 + o) * S : (9 + o) * S, :]
-        rmat[o * S : (o + 1) * S, :] = gj.astype(BF16)
-
-    for cp in f_copies:
-        cp.wait_recv()
-    total = fown[mr]
-    for i in range(1, R):
-        total = total + frecv[from_row(i)].astype(F32)
-    fm[...] = total
+        rmat[(o - 8) * S : (o - 7) * S, :] = gj.astype(BF16)
+
+    for c in range(FC):
+        f_copies[c].wait_recv()
+        cols = slice(c * 8 * E // FC, (c + 1) * 8 * E // FC)
+        fm[:, cols] += frecv[c].astype(F32)
     joined = jnp.concatenate([fm[:, o * E : (o + 1) * E] for o in range(8)], 0)
     cen = joined - jnp.mean(joined, -1, keepdims=True)
     inv_fm = lax.rsqrt(jnp.mean(cen * cen, -1, keepdims=True) + 1e-05)
@@ -452,28 +475,35 @@
     across = jnp.mean(up_fm * cen, -1, keepdims=True) * inv_fm
     grad_fm = (up_fm - up_mean - normed_fm * across) * inv_fm
     for o in range(8):
-        gf32[:, o * E : (o + 1) * E] = grad_fm[o * S : (o + 1) * S]
-    gall[mr] = gf32[...].astype(BF16)
-    g_copies = row_send(2, lambda p: gall.at[mr], gall)
+        gf32[:, o * E : (o + 1) * E] = grad_fm[o * 2 * S : (o + 1) * 2 * S]
+    gh = matmul(gf32[...].astype(BF16), wd[...], NT)
+    gp = (gh * ds[...]).astype(BF16)
+    q_copies = []
+    for c in range(QC):
+        cols = slice(c * K * T // QC, (c + 1) * K * T // QC)
+        part = matmul(gp, wp[cols, :], NT)
+        gq[:, cols] = part[0:S]
+        qsend[c] = part[S : 2 * S].astype(BF16)
+        q_copies.append(row_send(qsend.at[c], qrecv.at[c], 2 + FC + c))
     for o in range(8):
         lay32[:, o * E : (o + 1) * E] = (
-            normed_fm[o * S : (o + 1) * S] * gain_out + y[(8 + o) * S : (9 + o) * S, :]
+            normed_fm[o * 2 * S : (o * 2 + 1) * S] * gain_out + y[(8 + o) * S : (9 + o) * S, :]
         )
     lay_out[...] = lay32[...].astype(BF16)
-    for cp in g_copies:
-        cp.wait_recv()
-    gh = matmul(gall[...].reshape(R * S, 8 * E), wd[...], NT)
-    gp = (gh * ds[...]).astype(BF16)
-    gq = matmul(gp, wp[...], NT).reshape(R, S, K * T)
-    qsend[...] = gq.astype(BF16)
-    qown[...] = gq
-    q_copies = row_send(3, lambda p: qsend.at[p], qrecv)
-    for cp in q_copies:
-        cp.wait_recv()
-    gflat = qown[mr]
-    for i in range(1, R):
-        gflat = gflat + qrecv[from_row(i)].astype(F32)
-    qs = [gflat[:, k * T : (k + 1) * T] * gk[k : k + 1, :] for k in range(K)]
+    lge[...] = matmul(
+        lmask[:, :, 0:384].reshape(C * D * U, 384), rmat[0:384, :]
+    ).reshape(C, D * U, E)
+    for c in range(QC):
+        q_copies[c].wait_recv()
+    width = K // QC
+    qs = [
+        (
+            gq[:, k * T : (k + 1) * T]
+            + qrecv[k // width, :, k % width * T : (k % width + 1) * T].astype(F32)
+        )
+        * gk[k : k + 1, :]
+        for k in range(K)
+    ]
     ns = [nrm[k * S : (k + 1) * S, :] for k in range(K)]
     first = jnp.sum(sum(qs), -1, keepdims=True) / n_flat
     second = jnp.sum(sum(q * n for q, n in zip(qs, ns)), -1, keepdims=True) / n_flat
@@ -484,100 +514,88 @@
         lm[0:T, u * T : (u + 1) * T] = jnp.where(idx_t == float(u), gg, 0.0).astype(BF16)
     ggr[...] = gg.T
     fill(ggr, 4)
-    rmat[0:T, :] = matmul(lm[0:T, :], tst[...]).astype(BF16)
-    lg[...] = matmul(lmask[...], rmat[...])
-
-    top = lg[:, T:E].reshape(C, D * U, E - T)
-    sb[:, 64:96, :] = jnp.concatenate([top[:, :32], top[:, 32:]], -1).astype(BF16)
-    sb[:, 0:64, :] = lg[:, 0:T].reshape(C, D * U, T).astype(BF16)
-    cuts = (pl.ds(64, 32), pl.ds(0, 32), pl.ds(32, 32))
-    sems = ((sbs, rbs), (sa, ra), (sc, rc))
-    g_in = []
-
-    def send_lists(stage):
-        cut, (ssem, rsem) = cuts[stage], sems[stage]
-        g_in.append([])
-        for i in order:
-            p = to_col(i)
-            g_in[stage].append(
-                rcopy(sb.at[p, cut], rland.at[me, cut], ssem.at[i], rsem.at[i], {"col": p})
-            )
-            g_in[stage][-1].start()
-
-    send_lists(0)
-    send_lists(1)
+    rmat[384:512, :] = matmul(lm[0:T, :], tst[...]).astype(BF16)
+
+    units = []
+    for half in range(2):
+        at = half * 32
+        part = matmul(lmask[:, at : at + 32, 384:640].reshape(C * 32, 256), rmat[384:640, :])
+        part = part.reshape(C, 32, E) + lge[:, at : at + 32, :]
+        row = half * 48
+        top = part[:, :, T:E]
+        sb[:, row : row + 16, :] = jnp.concatenate([top[:, :16], top[:, 16:]], -1).astype(BF16)
+        sb[:, row + 16 : row + 48, :] = part[:, :, 0:T].astype(BF16)
+        for j in range(half * 3, half * 3 + 3):
+            cut = pl.ds(j * 16, 16)
+            units.append([])
+            for i in order:
+                p = to_col(i)
+                sem = j * C + i
+                units[j].append(
+                    rcopy(sb.at[p, cut], rland.at[me, cut], su.at[sem], ru.at[sem], {"col": p})
+                )
+                units[j][-1].start()
     rland[me] = sb[me]
 
     p_copies = []
-    for stage in range(3):
-        for cp in g_in[stage]:
+    for j in range(6):
+        for cp in units[j]:
             cp.wait_recv()
+        base, kind = j // 3 * 4, j % 3
+        both = rland[:, j * 16 : (j + 1) * 16, :].astype(F32)
         pieces = []
-        for p in range(2):
-            start = (64, 0, 32)[stage] + p * 16
-            both = rland[:, start : start + 16, :].astype(F32)
-            for h in range(2):
-                x = both[:, h * U : (h + 1) * U, :].reshape(T, T).T.astype(BF16)
-                d = 2 * p + h
-                if stage == 0:
-                    pieces.append((d, T, E, x[: E - T]))
-                    pieces.append((d + 4, T, E, x[E - T :]))
-                else:
-                    pieces.append((d + 4 * (stage - 1), 0, T, x))
-        for i in range(1, R):
-            for d, a, b, x in pieces:
-                ps[i, d, a:b, :] = matmul(x, oh[i, d], NT).astype(BF16)
-            part = (slice(0, D), slice(T, E)) if stage == 0 else (
-                slice(4 * (stage - 1), 4 * stage),
-                slice(0, T),
-            )
-            ds_of = tuple(pl.ds(q.start, q.stop - q.start) for q in part)
-            sem = (4 + stage) * R + i
-            p_copies.append(
-                rcopy(
-                    ps.at[(i,) + ds_of],
-                    pr.at[(i,) + ds_of],
-                    sx.at[sem],
-                    rx.at[sem],
-                    {"row": to_row(i)},
-                )
-            )
-            p_copies[-1].start()
-        if stage == 0:
-            send_lists(2)
+        for h in range(2):
+            x = both[:, h * U : (h + 1) * U, :].reshape(T, T).T.astype(BF16)
+            if kind == 0:
+                pieces.append((base + h, T, E, x[: E - T]))
+                pieces.append((base + 2 + h, T, E, x[E - T :]))
+            else:
+                pieces.append((base + 2 * (kind - 1) + h, 0, T, x))
+        for d, a, b, x in pieces:
+            ps[d, a:b, :] = matmul(x, oh[1, d], NT).astype(BF16)
+        if kind == 0:
+            part = (pl.ds(base, 4), pl.ds(T, E - T))
+        else:
+            part = (pl.ds(base + 2 * (kind - 1), 2), pl.ds(0, T))
+        p_copies.append(row_send(ps.at[part], pr.at[part], 2 + FC + QC + j))
         for d, a, b, x in pieces:
             rg_out[d, a:b, :] = matmul(x, oh[0, d], NT)
+    cp_m1.wait()
     for cp in p_copies:
         cp.wait_recv()
-    for i in range(1, R):
-        rg_out[...] += pr[i].astype(F32)
-
     for group in (
         idx_copies,
         row_copies,
-        n_copies,
+        [c_copy, n_copy],
         f_copies,
-        g_copies,
         q_copies,
-        g_in[0],
-        g_in[1],
-        g_in[2],
+        *units,
         p_copies,
     ):
         for cp in group:
             cp.wait_send()
 
 
-def moment_kernel(width, lay, grads, m1, m2, lay_out, m1_out, m2_out, step_out):
-    lay_out[...] = lay[...]
-    for h in range(4):
-        row = pl.ds(pl.program_id(0) * 4 + h, 1)
-        g = grads[h]
-        first = 0.9 * m1[h] + 0.1 * g
-        second = 0.99 * m2[row, :] + 0.01 * (jnp.sum(g * g, 0, keepdims=True) / width)
-        m1_out[h] = first
-        m2_out[row, :] = second
-        step_out[h] = first * lax.rsqrt(second)
+def moment_kernel(
+    width, lay, own, got, m1, m2, lay_out, m1_out, m2_out, step_out, mv, sv, m2v, sem
+):
+    D = own.shape[0]
+    copies = [pltpu.make_async_copy(lay, lay_out, sem.at[0])]
+    copies[0].start()
+    for d in range(D):
+        g = own[d] + got[d].astype(F32)
+        first = 0.9 * m1[d] + 0.1 * g
+        second = 0.99 * m2[d : d + 1, :] + 0.01 * (jnp.sum(g * g, 0, keepdims=True) / width)
+        mv[d] = first
+        m2v[d : d + 1, :] = second
+        sv[d] = first * lax.rsqrt(second)
+        for n, (a, b) in enumerate(((mv, m1_out), (sv, step_out))):
+            copies.append(pltpu.make_async_copy(a.at[d], b.at[d], sem.at[2 + 2 * d + n]))
+            copies[-1].start()
+    copies.append(pltpu.make_async_copy(m2v, m2_out, sem.at[1]))
+    copies[-1].start()
+    for cp in copies:
+        cp.wait()
 
 
 def fast_body(
@@ -607,15 +625,27 @@
     vmem = pl.BlockSpec(memory_space=pltpu.VMEM)
     hbm = pl.BlockSpec(memory_space=pl.ANY)
     dma = pltpu.SemaphoreType.DMA
-    layer_out, row_grads = pl.pallas_call(
-        functools.partial(fused_kernel, C, R, D),
+    layer_out, own, got, m1, m2 = pl.pallas_call(
+        functools.partial(fused_kernel, C, D),
         out_shape=(
-            jax.ShapeDtypeStruct((S, 16 * width), BF16),
-            jax.ShapeDtypeStruct((D, width, T), F32),
+            pltpu.VMEM((S, 16 * width), BF16),
+            pltpu.VMEM((D, width, T), F32),
+            pltpu.VMEM((D, width, T), BF16),
+            pltpu.VMEM((D, width, T), F32),
+            pltpu.VMEM((D, T), F32),
         ),
-        in_specs=[hbm, vmem, vmem, vmem, vmem, hbm, hbm, vmem, vmem, vmem, vmem],
-        out_specs=(vmem, vmem),
+        in_specs=[hbm] * 13,
+        out_specs=(vmem,) * 5,
         scratch_shapes=[
+            pltpu.VMEM((D, 8, C), jnp.int32),
+            pltpu.VMEM((D, C * S), jnp.int32),
+            pltpu.VMEM((8, T), BF16),
+            pltpu.VMEM((1, flat), F32),
+            pltpu.VMEM((8, T), BF16),
+            pltpu.VMEM((16, T), BF16),
+            pltpu.VMEM((1, width), F32),
+            pltpu.VMEM((S, 16 * width), BF16),
+            pltpu.VMEM((S, wide), BF16),
             pltpu.VMEM((C, D, S), jnp.int32),
             pltpu.VMEM((C, D, wide), BF16),
             pltpu.VMEM((C, D, S), jnp.int32),
@@ -625,78 +655,85 @@
             pltpu.VMEM((T, wide), F32),
             pltpu.VMEM((8 * T, width), BF16),
             pltpu.VMEM((512, 8 * T), BF16),
-            pltpu.VMEM((8 * T, 640), BF16),
+            pltpu.VMEM((C, 8 * D, 640), BF16),
             pltpu.VMEM((512, T), F32),
             pltpu.VMEM((640, width), BF16),
             pltpu.VMEM((128, T), F32),
             pltpu.VMEM((128, T), F32),
             pltpu.VMEM((T, 128), F32),
-            pltpu.VMEM((R, S, flat), BF16),
+            pltpu.VMEM((2, S, flat), BF16),
             pltpu.VMEM((384, width), F32),
-            pltpu.VMEM((R * S, hid), F32),
-            pltpu.VMEM((R, S, wide), F32),
-            pltpu.VMEM((R, S, wide), BF16),
-            pltpu.VMEM((R, S, wide), BF16),
-            pltpu.VMEM((S, wide), F32),
-            pltpu.VMEM((R, S, wide), BF16),
-            pltpu.VMEM((R, S, flat), F32),
-            pltpu.VMEM((R, S, flat), BF16),
-            pltpu.VMEM((R, S, flat), BF16),
+            pltpu.VMEM((2 * S, hid), F32),
+            pltpu.VMEM((2 * S, wide), F32),
+            pltpu.VMEM((3, 2 * S, wide // 3), BF16),
+            pltpu.VMEM((3, 2 * S, wide // 3), BF16),
+            pltpu.VMEM((2 * S, wide), F32),
+            pltpu.VMEM((2, S, flat // 2), BF16),
+            pltpu.VMEM((2, S, flat // 2), BF16),
+            pltpu.VMEM((S, flat), F32),
             pltpu.VMEM((S, 16 * width), F32),
-            pltpu.VMEM((S, wide), F32),
-            pltpu.VMEM((8 * T, width), F32),
+            pltpu.VMEM((2 * S, wide), F32),
+            pltpu.VMEM((C, 8 * D, width), F32),
             pltpu.VMEM((C, 12 * D, T), BF16),
             pltpu.VMEM((C, 12 * D, T), BF16),
-            pltpu.VMEM((R, D, T, T), BF16),
-            pltpu.VMEM((R, D, width, T), BF16),
-            pltpu.VMEM((R, D, width, T), BF16),
-            dma((4,)),
+            pltpu.VMEM((2, D, T, T), BF16),
+            pltpu.VMEM((D, width, T), BF16),
+            dma((13,)),
             dma((C,)),
             dma((C,)),
             dma((C,)),
             dma((C,)),
-            dma((C,)),
-            dma((C,)),
-            dma((C,)),
-            dma((C,)),
-            dma((C,)),
-            dma((C,)),
-            dma((7 * R,)),
-            dma((7 * R,)),
+            dma((6 * C,)),
+            dma((6 * C,)),
+            dma((13,)),
+            dma((13,)),
         ],
         compiler_params=pltpu.CompilerParams(
-            collective_id=0, has_side_effects=True, vmem_limit_bytes=56 * 1024 * 1024
+            collective_id=0, has_side_effects=True, vmem_limit_bytes=36 * 1024 * 1024
         ),
         name="wukong_step",
     )(
-        uniq_rows,
-        row_ids.transpose(1, 2, 0),
-        sample_idx.T,
-        fm_proj.T,
-        ln_gain.reshape(1, flat),
-        w_up,
-        w_down,
-        w_lc,
-        w_res,
-        out_gain.reshape(1, width),
-        cotangent,
-    )
-    slab = pl.BlockSpec((4, width, T), lambda d: (d, 0, 0))
-    whole = pl.BlockSpec((D, T), lambda d: (0, 0))
-    strip = pl.BlockSpec((S, 8 * width), lambda d: (0, d))
+        *(
+            pltpu.with_memory_space_constraint(a, pltpu.HBM)
+            for a in (
+                uniq_rows,
+                row_ids.transpose(1, 2, 0),
+                sample_idx.T,
+                fm_proj.T,
+                ln_gain.reshape(1, flat),
+                w_up,
+                w_down,
+                w_lc,
+                w_res,
+                out_gain.reshape(1, width),
+                cotangent,
+                moment1.transpose(0, 2, 1),
+                moment2,
+            )
+        )
+    )
+    layer_out, own, got, m1, m2 = (
+        pltpu.with_memory_space_constraint(a, pltpu.VMEM) for a in (layer_out, own, got, m1, m2)
+    )
     layer_out, new_moment1, new_moment2, row_step = pl.pallas_call(
         functools.partial(moment_kernel, width),
-        grid=(D // 4,),
         out_shape=(
             jax.ShapeDtypeStruct((S, 16 * width), BF16),
             jax.ShapeDtypeStruct((D, width, T), F32),
             jax.ShapeDtypeStruct((D, T), F32),
             jax.ShapeDtypeStruct((D, width, T), F32),
         ),
-        in_specs=[strip, slab, slab, whole],
-        out_specs=(strip, slab, whole, slab),
+        in_specs=[vmem] * 5,
+        out_specs=(hbm,) * 4,
+        scratch_shapes=[
+            pltpu.VMEM((D, width, T), F32),
+            pltpu.VMEM((D, width, T), F32),
+            pltpu.VMEM((D, T), F32),
+            dma((2 + 2 * D,)),
+        ],
+        compiler_params=pltpu.CompilerParams(vmem_limit_bytes=8 * 1024 * 1024),
         name="moments",
-    )(layer_out, row_grads, moment1.transpose(0, 2, 1), moment2)
+    )(layer_out, own, got, m1, m2)
     return (
         layer_out,
         new_moment1.transpose(0, 2, 1),
@@ -706,7 +743,7 @@
 
 
 def step(C, R, *args):
-    if args[0].shape[1] == 8 and C == 16:
+    if args[0].shape[1] == 8 and C == 16 and R == 2:
         return fast_body(C, R, *args)
     return plain_body(*args)
 

time: 57.7 us -> 52.2 us (0.905)
  Pallas kernels: 56.8 us -> 51.3 us
    pallas_call x2, Pallas kernels: 56.8 us -> 51.3 us  [the longest x1 50 us: fast_body(): pl.pallas_call(functools.partial(fused_kernel, C, D), out_shape=(pltpu.VM...]
where the time goes in v1:
time: 52.2 us; the launch traced here: 52 us
  Pallas kernels  51.3 us (98%)
  between operations  0.64 us (1%)
    pallas_call x1, Pallas kernels, fast_body(): pl.pallas_call(functools.partial(fused_kernel, C, D), out_shape=(pltpu.VM...  50 us
    pallas_call x1, Pallas kernels, fast_body(): pl.pallas_call(functools.partial(moment_kernel, width), out_shape=(jax.Sh...  1.32 us

profile of v1, /device:TPU:0, one launch (start us, length us, event | category | flops | bytes accessed | tf_op | source)
XLA Modules:
  0.0 52.0 jit_solution(4410127550692398437)
XLA Ops:
  0.6 50.0 %wukong_step.1 = (bf16[16,3072]{1,0:T(8,128)(2,1)S(1)}, f32[8,192,128]{2,1,0:T(8,128)S(1)}, bf16[8,192,128]{2,1,0:T(8,128)(2,1)S(1)}, f32[8,192,128]{2,1,0:T(8,128)S(1)}, f32[8,128]{1,0:T(8,128)S(1)}) custom-call(bf16[16,8,1536]{2,1,0:T(8,128)(2,1)} %uniq.1, s32[8,8,16]{2,1,0:T(8,128)} %bitcast.9, s32[8,256]{1,0:T(8,128)} %bitcast.10, ...), custom_call_target="tpu_custom_call" | custom-call | tf_op jit(solution)/shard_map/wukong_step/pallas_call | solution.py:628
  50.6 1.3 %moments.1 = (bf16[16,3072]{1,0:T(8,128)(2,1)}, f32[8,192,128]{2,1,0:T(8,128)}, f32[8,128]{1,0:T(8,128)}, f32[8,192,128]{2,1,0:T(8,128)}) custom-call(bf16[16,3072]{1,0:T(8,128)(2,1)S(1)} %get-tuple-element.13.lay, f32[8,192,128]{2,1,0:T(8,128)S(1)} %get-tuple-element.14.own, bf16[8,192,128]{2,1,0:T(8,128)(2,1)S(1)} %get-tuple-element.15.got, ...), custom_call_target="tpu_custom_call" | custom-call | tf_op jit(solution)/shard_map/moments/pallas_call | solution.py:718

commit v2 on v1

--- a/solution.py
+++ b/solution.py
@@ -203,7 +203,6 @@
     m1_out,
     m2_out,
     rid,
-    sidx,
     fmp,
     gain,
     wlc,
@@ -211,7 +210,6 @@
     og,
     cot,
     cpeer,
-    isend,
     land,
     iland,
     wraw,
@@ -244,17 +242,13 @@
     oh,
     ps,
     loc,
-    s1,
-    r1,
-    si,
-    ri,
-    su,
-    ru,
+    sa,
+    ra,
     sx,
     rx,
 ):
     S, E, U, K, T = 16, 192, 8, 8, 128
-    FC, QC = 3, 2
+    FC, QC, PACE = 2, 2, 0
     me = lax.axis_index("col")
     mr = lax.axis_index("row")
     other = 1 - mr
@@ -285,8 +279,9 @@
     pl.semaphore_signal(
         barrier, inc=1, device_id={"row": other}, device_id_type=pl.DeviceIdType.MESH
     )
-    cp_idx = pltpu.make_async_copy(sidx_in, sidx, loc.at[0])
-    cp_idx.start()
+    tile = lambda p: sidx_in.at[:, pl.ds(pl.multiple_of(p * S // T * T, T), T)]
+    own_idx = pltpu.make_async_copy(tile(me), iland.at[me], loc.at[0])
+    own_idx.start()
     cp_up = pltpu.make_async_copy(wup, wraw, loc.at[1])
     cp_dn = pltpu.make_async_copy(wdn, wd, loc.at[2])
     own_rows = pltpu.make_async_copy(uniq.at[me], land.at[me], loc.at[3])
@@ -312,26 +307,18 @@
     cp_up.start()
     cp_dn.start()
     cp_m1.start()
-    cp_idx.wait()
-    for p in range(C):
-        at = p * S % T
-        tile = sidx[:, p * S // T * T : (p * S // T + 1) * T]
-        if at:
-            tile = pltpu.roll(tile, T - at, 1)
-        isend[p] = tile[:, :S]
-    iland[me] = isend[me]
     pl.semaphore_wait(barrier, C)
 
     order = sorted(range(1, C), key=lambda i: -min(i, C - i))
-    idx_copies, row_copies = [], []
     for i in order:
         p = to_col(i)
-        idx_copies.append(rcopy(isend.at[p], iland.at[me], si.at[i], ri.at[i], {"col": p}))
-        idx_copies[-1].start()
+        rcopy(tile(p), iland.at[me], sa.at[0], ra.at[0], {"col": p}).start()
     for i in order:
         p = to_col(i)
-        row_copies.append(rcopy(uniq.at[p], land.at[me], s1.at[i], r1.at[i], {"col": p}))
-        row_copies[-1].start()
+        rcopy(uniq.at[p], land.at[me], sa.at[1], ra.at[1], {"col": p}).start()
+    most = pl.ds(0, C - 1)
+    all_idx = rcopy(iland.at[most], iland.at[most], sa.at[0], ra.at[0], {"row": other})
+    all_rows = rcopy(land.at[most], land.at[most], sa.at[1], ra.at[1], {"row": other})
     c_copy = row_send(cot_in.at[:, pl.ds(0, 8 * E)], cpeer, 0)
 
     to, at = iota((256, 256), 0), iota((256, 256), 1)
@@ -371,10 +358,11 @@
                 target == jnp.broadcast_to(local[d : d + 1, :], (T, T)), 1.0, 0.0
             ).astype(BF16)
 
-    for cp in idx_copies:
-        cp.wait_recv()
-    ix = iland[...].astype(F32).reshape(T, S)
-    tiled = (iota((S, T), 0) == (iota((S, T), 1) & (S - 1))).astype(F32)
+    own_idx.wait()
+    all_idx.wait_recv()
+    ix = iland[...].astype(F32).reshape(T, T)
+    mine = lax.rem(me, T // S) * S
+    tiled = (iota((T, T), 0) == (iota((T, T), 1) & (S - 1)) + mine).astype(F32)
     idx_n = matmul(ix, tiled, precision=HIGH)
     idxn[...] = idx_n
     idx_t = idx_n.T
@@ -385,8 +373,8 @@
             ).astype(BF16)
     entry = iota((U, T), 0).astype(F32)
 
-    def fill(src, at):
-        for t in range(0, T, 2):
+    def fill(src, at, slots=range(0, T, 2)):
+        for t in slots:
             rows = [
                 jnp.where(
                     jnp.broadcast_to(idxn[v : v + 1, :], (U, T)) == entry,
@@ -407,8 +395,7 @@
         rmat[(8 + o) * S : (9 + o) * S, :] = upstream[:, o * E : (o + 1) * E].astype(BF16)
 
     own_rows.wait()
-    for cp in row_copies:
-        cp.wait_recv()
+    all_rows.wait_recv()
     t32[...] = land[...].astype(F32).reshape(T, U * E)
     for u in range(U):
         tst[u * T : (u + 1) * T, :] = t32[:, u * E : (u + 1) * E].astype(BF16)
@@ -464,19 +451,27 @@
         lay32[:, o * E : (o + 1) * E] = nr * gain_out + y[(8 + o) * S : (9 + o) * S, :]
         rmat[(o - 8) * S : (o - 7) * S, :] = gj.astype(BF16)
 
+    normed_fm, gh = [], None
+    per = 8 // FC
     for c in range(FC):
         f_copies[c].wait_recv()
-        cols = slice(c * 8 * E // FC, (c + 1) * 8 * E // FC)
+        cols = slice(c * per * E, (c + 1) * per * E)
+        rows = slice(c * per * 2 * S, (c + 1) * per * 2 * S)
         fm[:, cols] += frecv[c].astype(F32)
-    joined = jnp.concatenate([fm[:, o * E : (o + 1) * E] for o in range(8)], 0)
-    cen = joined - jnp.mean(joined, -1, keepdims=True)
-    inv_fm = lax.rsqrt(jnp.mean(cen * cen, -1, keepdims=True) + 1e-05)
-    normed_fm = cen * inv_fm
-    across = jnp.mean(up_fm * cen, -1, keepdims=True) * inv_fm
-    grad_fm = (up_fm - up_mean - normed_fm * across) * inv_fm
-    for o in range(8):
-        gf32[:, o * E : (o + 1) * E] = grad_fm[o * 2 * S : (o + 1) * 2 * S]
-    gh = matmul(gf32[...].astype(BF16), wd[...], NT)
+        joined = jnp.concatenate(
+            [fm[:, o * E : (o + 1) * E] for o in range(c * per, (c + 1) * per)], 0
+        )
+        cen = joined - jnp.mean(joined, -1, keepdims=True)
+        inv_fm = lax.rsqrt(jnp.mean(cen * cen, -1, keepdims=True) + 1e-05)
+        normed = cen * inv_fm
+        across = jnp.mean(up_fm[rows] * cen, -1, keepdims=True) * inv_fm
+        grad_fm = (up_fm[rows] - up_mean[rows] - normed * across) * inv_fm
+        for o in range(per):
+            at = (c * per + o) * E
+            gf32[:, at : at + E] = grad_fm[o * 2 * S : (o + 1) * 2 * S]
+            normed_fm.append(normed[o * 2 * S : o * 2 * S + S])
+        part = matmul(gf32[:, cols].astype(BF16), wd[:, cols], NT)
+        gh = part if gh is None else gh + part
     gp = (gh * ds[...]).astype(BF16)
     q_copies = []
     for c in range(QC):
@@ -487,7 +482,7 @@
         q_copies.append(row_send(qsend.at[c], qrecv.at[c], 2 + FC + c))
     for o in range(8):
         lay32[:, o * E : (o + 1) * E] = (
-            normed_fm[o * 2 * S : (o * 2 + 1) * S] * gain_out + y[(8 + o) * S : (9 + o) * S, :]
+            normed_fm[o] * gain_out + y[(8 + o) * S : (9 + o) * S, :]
         )
     lay_out[...] = lay32[...].astype(BF16)
     lge[...] = matmul(
@@ -513,12 +508,12 @@
     for u in range(U):
         lm[0:T, u * T : (u + 1) * T] = jnp.where(idx_t == float(u), gg, 0.0).astype(BF16)
     ggr[...] = gg.T
-    fill(ggr, 4)
     rmat[384:512, :] = matmul(lm[0:T, :], tst[...]).astype(BF16)
 
     units = []
     for half in range(2):
         at = half * 32
+        fill(ggr, 4, [t for t in range(0, T, 2) if t % D // 4 == half])
         part = matmul(lmask[:, at : at + 32, 384:640].reshape(C * 32, 256), rmat[384:640, :])
         part = part.reshape(C, 32, E) + lge[:, at : at + 32, :]
         row = half * 48
@@ -526,21 +521,24 @@
         sb[:, row : row + 16, :] = jnp.concatenate([top[:, :16], top[:, 16:]], -1).astype(BF16)
         sb[:, row + 16 : row + 48, :] = part[:, :, 0:T].astype(BF16)
         for j in range(half * 3, half * 3 + 3):
+            if PACE and j >= PACE:
+                units[j - PACE].wait_send()
             cut = pl.ds(j * 16, 16)
-            units.append([])
             for i in order:
                 p = to_col(i)
-                sem = j * C + i
-                units[j].append(
-                    rcopy(sb.at[p, cut], rland.at[me, cut], su.at[sem], ru.at[sem], {"col": p})
+                rcopy(
+                    sb.at[p, cut], rland.at[me, cut], sa.at[2 + j], ra.at[2 + j], {"col": p}
+                ).start()
+            units.append(
+                rcopy(
+                    sb.at[most, cut], rland.at[most, cut], sa.at[2 + j], ra.at[2 + j], {"row": other}
                 )
-                units[j][-1].start()
+            )
     rland[me] = sb[me]
 
     p_copies = []
     for j in range(6):
-        for cp in units[j]:
-            cp.wait_recv()
+        units[j].wait_recv()
         base, kind = j // 3 * 4, j % 3
         both = rland[:, j * 16 : (j + 1) * 16, :].astype(F32)
         pieces = []
@@ -563,17 +561,17 @@
     cp_m1.wait()
     for cp in p_copies:
         cp.wait_recv()
-    for group in (
-        idx_copies,
-        row_copies,
-        [c_copy, n_copy],
-        f_copies,
-        q_copies,
-        *units,
-        p_copies,
+    for cp in (
+        all_idx,
+        all_rows,
+        c_copy,
+        n_copy,
+        *f_copies,
+        *q_copies,
+        *(units[6 - PACE :] if PACE else units),
+        *p_copies,
     ):
-        for cp in group:
-            cp.wait_send()
+        cp.wait_send()
 
 
 def moment_kernel(
@@ -638,7 +636,6 @@
         out_specs=(vmem,) * 5,
         scratch_shapes=[
             pltpu.VMEM((D, 8, C), jnp.int32),
-            pltpu.VMEM((D, C * S), jnp.int32),
             pltpu.VMEM((8, T), BF16),
             pltpu.VMEM((1, flat), F32),
             pltpu.VMEM((8, T), BF16),
@@ -646,9 +643,8 @@
             pltpu.VMEM((1, width), F32),
             pltpu.VMEM((S, 16 * width), BF16),
             pltpu.VMEM((S, wide), BF16),
-            pltpu.VMEM((C, D, S), jnp.int32),
             pltpu.VMEM((C, D, wide), BF16),
-            pltpu.VMEM((C, D, S), jnp.int32),
+            pltpu.VMEM((C, D, T), jnp.int32),
             pltpu.VMEM((flat, hid), BF16),
             pltpu.VMEM((flat, hid), BF16),
             pltpu.VMEM((hid, wide), BF16),
@@ -665,8 +661,8 @@
             pltpu.VMEM((384, width), F32),
             pltpu.VMEM((2 * S, hid), F32),
             pltpu.VMEM((2 * S, wide), F32),
-            pltpu.VMEM((3, 2 * S, wide // 3), BF16),
-            pltpu.VMEM((3, 2 * S, wide // 3), BF16),
+            pltpu.VMEM((2, 2 * S, wide // 2), BF16),
+            pltpu.VMEM((2, 2 * S, wide // 2), BF16),
             pltpu.VMEM((2 * S, wide), F32),
             pltpu.VMEM((2, S, flat // 2), BF16),
             pltpu.VMEM((2, S, flat // 2), BF16),
@@ -679,12 +675,8 @@
             pltpu.VMEM((2, D, T, T), BF16),
             pltpu.VMEM((D, width, T), BF16),
             dma((13,)),
-            dma((C,)),
-            dma((C,)),
-            dma((C,)),
-            dma((C,)),
-            dma((6 * C,)),
-            dma((6 * C,)),
+            dma((8,)),
+            dma((8,)),
             dma((13,)),
             dma((13,)),
         ],

time: 52.2 us -> 49.9 us (0.956)
  Pallas kernels: 51.3 us -> 49.1 us
    pallas_call x1, Pallas kernels: 50 us -> 47.8 us  [fast_body(): pl.pallas_call(functools.partial(fused_kernel, C, D), out_shape=(pltpu.VM...]
where the time goes in v2:
time: 49.9 us; the launch traced here: 49.8 us
  Pallas kernels  49.1 us (98%)
  between operations  0.64 us (1%)
    pallas_call x1, Pallas kernels, fast_body(): pl.pallas_call(functools.partial(fused_kernel, C, D), out_shape=(pltpu.VM...  47.8 us
    pallas_call x1, Pallas kernels, fast_body(): pl.pallas_call(functools.partial(moment_kernel, width), out_shape=(jax.Sh...  1.32 us

profile of v2, /device:TPU:0, one launch (start us, length us, event | category | flops | bytes accessed | tf_op | source)
XLA Modules:
  0.0 49.8 jit_solution(17343354250145255479)
XLA Ops:
  0.6 47.8 %wukong_step.1 = (bf16[16,3072]{1,0:T(8,128)(2,1)S(1)}, f32[8,192,128]{2,1,0:T(8,128)S(1)}, bf16[8,192,128]{2,1,0:T(8,128)(2,1)S(1)}, f32[8,192,128]{2,1,0:T(8,128)S(1)}, f32[8,128]{1,0:T(8,128)S(1)}) custom-call(bf16[16,8,1536]{2,1,0:T(8,128)(2,1)} %uniq.1, s32[8,8,16]{2,1,0:T(8,128)} %bitcast.9, s32[8,256]{1,0:T(8,128)} %bitcast.10, ...), custom_call_target="tpu_custom_call" | custom-call | tf_op jit(solution)/shard_map/wukong_step/pallas_call | solution.py:626
  48.4 1.3 %moments.1 = (bf16[16,3072]{1,0:T(8,128)(2,1)}, f32[8,192,128]{2,1,0:T(8,128)}, f32[8,128]{1,0:T(8,128)}, f32[8,192,128]{2,1,0:T(8,128)}) custom-call(bf16[16,3072]{1,0:T(8,128)(2,1)S(1)} %get-tuple-element.13.lay, f32[8,192,128]{2,1,0:T(8,128)S(1)} %get-tuple-element.14.own, bf16[8,192,128]{2,1,0:T(8,128)(2,1)S(1)} %get-tuple-element.15.got, ...), custom_call_target="tpu_custom_call" | custom-call | tf_op jit(solution)/shard_map/moments/pallas_call | solution.py:710

commit v3 on v2

--- a/solution.py
+++ b/solution.py
@@ -241,6 +241,10 @@
     rland,
     oh,
     ps,
+    ridp,
+    yb,
+    rlandp,
+    ohp,
     loc,
     sa,
     ra,
@@ -248,7 +252,7 @@
     rx,
 ):
     S, E, U, K, T = 16, 192, 8, 8, 128
-    FC, QC, PACE = 2, 2, 0
+    FC, QC = 2, 2
     me = lax.axis_index("col")
     mr = lax.axis_index("row")
     other = 1 - mr
@@ -320,6 +324,7 @@
     all_idx = rcopy(iland.at[most], iland.at[most], sa.at[0], ra.at[0], {"row": other})
     all_rows = rcopy(land.at[most], land.at[most], sa.at[1], ra.at[1], {"row": other})
     c_copy = row_send(cot_in.at[:, pl.ds(0, 8 * E)], cpeer, 0)
+    rid_copy = row_send(rid_in, ridp, 12)
 
     to, at = iota((256, 256), 0), iota((256, 256), 1)
     perm = (((to & 31) * 8 + (to >> 5)) == at).astype(F32).astype(BF16)
@@ -347,9 +352,13 @@
         arep[j * S : (j + 1) * S, :] = jnp.broadcast_to(amat[j : j + 1, :], (S, T))
 
     place = (iota((C, T), 0) == (iota((C, T), 1) >> 3)).astype(F32)
-    wide = matmul(rid[...].astype(F32).reshape(D * U, C), place, precision=HIGH).reshape(D, U, T)
-    mine = iota((D, U, T), 1) == (iota((D, U, T), 2) & (U - 1))
-    labels = jnp.sum(jnp.where(mine, wide, 0.0), 1).astype(jnp.int32)
+    same = iota((D, U, T), 1) == (iota((D, U, T), 2) & (U - 1))
+
+    def labels_of(ids):
+        wide = matmul(ids[...].astype(F32).reshape(D * U, C), place, precision=HIGH)
+        return jnp.sum(jnp.where(same, wide.reshape(D, U, T), 0.0), 1).astype(jnp.int32)
+
+    labels = labels_of(rid)
     target = iota((T, T), 0)
     for i in range(2):
         local = labels - (mr if i == 0 else other) * T
@@ -394,6 +403,13 @@
     for o in range(16):
         rmat[(8 + o) * S : (9 + o) * S, :] = upstream[:, o * E : (o + 1) * E].astype(BF16)
 
+    rid_copy.wait_recv()
+    local = labels_of(ridp) - mr * T
+    for d in range(4):
+        ohp[d] = jnp.where(
+            target == jnp.broadcast_to(local[d + 4 : d + 5, :], (T, T)), 1.0, 0.0
+        ).astype(BF16)
+    pr[4:D, 0:T, :] = jnp.zeros((4, T, T), BF16)
     own_rows.wait()
     all_rows.wait_recv()
     t32[...] = land[...].astype(F32).reshape(T, U * E)
@@ -511,7 +527,23 @@
     rmat[384:512, :] = matmul(lm[0:T, :], tst[...]).astype(BF16)
 
     units = []
-    for half in range(2):
+
+    def col_send(src, dst, sem):
+        for i in order:
+            p = to_col(i)
+            rcopy(src(p), dst, sa.at[sem], ra.at[sem], {"col": p}).start()
+
+    def unit_send(j, row):
+        cut = pl.ds(row, 16)
+        col_send(lambda p: sb.at[p, cut], rland.at[me, cut], 2 + j)
+        units.append(
+            rcopy(
+                sb.at[most, cut], rland.at[most, cut], sa.at[2 + j], ra.at[2 + j], {"row": other}
+            )
+        )
+
+    y_copies = []
+    for half in (1, 0):
         at = half * 32
         fill(ggr, 4, [t for t in range(0, T, 2) if t % D // 4 == half])
         part = matmul(lmask[:, at : at + 32, 384:640].reshape(C * 32, 256), rmat[384:640, :])
@@ -520,44 +552,66 @@
         top = part[:, :, T:E]
         sb[:, row : row + 16, :] = jnp.concatenate([top[:, :16], top[:, 16:]], -1).astype(BF16)
         sb[:, row + 16 : row + 48, :] = part[:, :, 0:T].astype(BF16)
-        for j in range(half * 3, half * 3 + 3):
-            if PACE and j >= PACE:
-                units[j - PACE].wait_send()
-            cut = pl.ds(j * 16, 16)
-            for i in order:
-                p = to_col(i)
-                rcopy(
-                    sb.at[p, cut], rland.at[me, cut], sa.at[2 + j], ra.at[2 + j], {"col": p}
-                ).start()
-            units.append(
-                rcopy(
-                    sb.at[most, cut], rland.at[most, cut], sa.at[2 + j], ra.at[2 + j], {"row": other}
+        if half:
+            for c in range(2):
+                y_copies.append(
+                    row_send(
+                        sb.at[:, pl.ds(64 + c * 16, 16)], yb.at[:, pl.ds(c * 16, 16)], 10 + c
+                    )
                 )
-            )
+            unit_send(0, 48)
+        else:
+            for j in range(3):
+                unit_send(1 + j, j * 16)
+    late = pl.ds(64, 32)
+    col_send(lambda p: sb.at[p, late], rland.at[me, late], 6)
+    lists = [
+        rcopy(sb.at[most, late], rland.at[most, late], sa.at[6], ra.at[6], {"row": other})
+    ]
     rland[me] = sb[me]
 
+    def relay(c):
+        y_copies[c].wait_recv()
+        cut = pl.ds(c * 16, 16)
+        col_send(lambda p: yb.at[p, cut], rlandp.at[me, cut], 7 + c)
+        rlandp[me, c * 16 : (c + 1) * 16, :] = yb[me, c * 16 : (c + 1) * 16, :]
+        lists.append(
+            rcopy(yb.at[most, cut], rlandp.at[most, cut], sa.at[7 + c], ra.at[7 + c], {"row": other})
+        )
+
+    def halves(ref, row):
+        both = ref[:, row : row + 16, :].astype(F32)
+        return [both[:, h * U : (h + 1) * U, :].reshape(T, T).T.astype(BF16) for h in range(2)]
+
     p_copies = []
-    for j in range(6):
+    for j in range(4):
+        if j < 2:
+            relay(j)
         units[j].wait_recv()
-        base, kind = j // 3 * 4, j % 3
-        both = rland[:, j * 16 : (j + 1) * 16, :].astype(F32)
+        base, row = ((4, 48), (0, 0), (0, 16), (2, 32))[j]
         pieces = []
-        for h in range(2):
-            x = both[:, h * U : (h + 1) * U, :].reshape(T, T).T.astype(BF16)
-            if kind == 0:
+        for h, x in enumerate(halves(rland, row)):
+            if j < 2:
                 pieces.append((base + h, T, E, x[: E - T]))
                 pieces.append((base + 2 + h, T, E, x[E - T :]))
             else:
-                pieces.append((base + 2 * (kind - 1) + h, 0, T, x))
+                pieces.append((base + h, 0, T, x))
         for d, a, b, x in pieces:
             ps[d, a:b, :] = matmul(x, oh[1, d], NT).astype(BF16)
-        if kind == 0:
-            part = (pl.ds(base, 4), pl.ds(T, E - T))
-        else:
-            part = (pl.ds(base + 2 * (kind - 1), 2), pl.ds(0, T))
+        part = (pl.ds(base, 4), pl.ds(T, E - T)) if j < 2 else (pl.ds(base, 2), pl.ds(0, T))
         p_copies.append(row_send(ps.at[part], pr.at[part], 2 + FC + QC + j))
         for d, a, b, x in pieces:
             rg_out[d, a:b, :] = matmul(x, oh[0, d], NT)
+    lists[0].wait_recv()
+    for c in range(2):
+        for h, x in enumerate(halves(rland, 64 + c * 16)):
+            d = 4 + 2 * c + h
+            rg_out[d, 0:T, :] = matmul(x, oh[0, d], NT)
+    for c in range(2):
+        lists[1 + c].wait_recv()
+        for h, x in enumerate(halves(rlandp, c * 16)):
+            d = 4 + 2 * c + h
+            rg_out[d, 0:T, :] += matmul(x, ohp[d - 4], NT)
     cp_m1.wait()
     for cp in p_copies:
         cp.wait_recv()
@@ -568,7 +622,10 @@
         n_copy,
         *f_copies,
         *q_copies,
-        *(units[6 - PACE :] if PACE else units),
+        rid_copy,
+        *units,
+        *y_copies,
+        *lists,
         *p_copies,
     ):
         cp.wait_send()
@@ -674,9 +731,13 @@
             pltpu.VMEM((C, 12 * D, T), BF16),
             pltpu.VMEM((2, D, T, T), BF16),
             pltpu.VMEM((D, width, T), BF16),
+            pltpu.VMEM((D, 8, C), jnp.int32),
+            pltpu.VMEM((C, 4 * D, T), BF16),
+            pltpu.VMEM((C, 4 * D, T), BF16),
+            pltpu.VMEM((4, T, T), BF16),
             dma((13,)),
-            dma((8,)),
-            dma((8,)),
+            dma((9,)),
+            dma((9,)),
             dma((13,)),
             dma((13,)),
         ],

time: 49.9 us -> 47.1 us (0.944)
  Pallas kernels: 49.1 us -> 46.3 us
    pallas_call x1, Pallas kernels: 47.8 us -> 45 us  [fast_body(): pl.pallas_call(functools.partial(fused_kernel, C, D), out_shape=(pltpu.VM...]
where the time goes in v3:
time: 47.1 us; the launch traced here: 47 us
  Pallas kernels  46.3 us (98%)
  between operations  0.64 us (1%)
    pallas_call x1, Pallas kernels, fast_body(): pl.pallas_call(functools.partial(fused_kernel, C, D), out_shape=(pltpu.VM...  45 us
    pallas_call x1, Pallas kernels, fast_body(): pl.pallas_call(functools.partial(moment_kernel, width), out_shape=(jax.Sh...  1.32 us

profile of v3, /device:TPU:0, one launch (start us, length us, event | category | flops | bytes accessed | tf_op | source)
XLA Modules:
  0.0 47.0 jit_solution(17263228746731029861)
XLA Ops:
  0.6 45.0 %wukong_step.1 = (bf16[16,3072]{1,0:T(8,128)(2,1)S(1)}, f32[8,192,128]{2,1,0:T(8,128)S(1)}, bf16[8,192,128]{2,1,0:T(8,128)(2,1)S(1)}, f32[8,192,128]{2,1,0:T(8,128)S(1)}, f32[8,128]{1,0:T(8,128)S(1)}) custom-call(bf16[16,8,1536]{2,1,0:T(8,128)(2,1)} %uniq.1, s32[8,8,16]{2,1,0:T(8,128)} %bitcast.9, s32[8,256]{1,0:T(8,128)} %bitcast.10, ...), custom_call_target="tpu_custom_call" | custom-call | tf_op jit(solution)/shard_map/wukong_step/pallas_call | solution.py:683
  45.7 1.3 %moments.1 = (bf16[16,3072]{1,0:T(8,128)(2,1)}, f32[8,192,128]{2,1,0:T(8,128)}, f32[8,128]{1,0:T(8,128)}, f32[8,192,128]{2,1,0:T(8,128)}) custom-call(bf16[16,3072]{1,0:T(8,128)(2,1)S(1)} %get-tuple-element.13.lay, f32[8,192,128]{2,1,0:T(8,128)S(1)} %get-tuple-element.14.own, bf16[8,192,128]{2,1,0:T(8,128)(2,1)S(1)} %get-tuple-element.15.got, ...), custom_call_target="tpu_custom_call" | custom-call | tf_op jit(solution)/shard_map/moments/pallas_call | solution.py:771

commit v4 on v3

--- a/solution.py
+++ b/solution.py
@@ -203,6 +203,7 @@
     m1_out,
     m2_out,
     rid,
+    sidx,
     fmp,
     gain,
     wlc,
@@ -210,6 +211,7 @@
     og,
     cot,
     cpeer,
+    isend,
     land,
     iland,
     wraw,
@@ -283,9 +285,8 @@
     pl.semaphore_signal(
         barrier, inc=1, device_id={"row": other}, device_id_type=pl.DeviceIdType.MESH
     )
-    tile = lambda p: sidx_in.at[:, pl.ds(pl.multiple_of(p * S // T * T, T), T)]
-    own_idx = pltpu.make_async_copy(tile(me), iland.at[me], loc.at[0])
-    own_idx.start()
+    cp_idx = pltpu.make_async_copy(sidx_in, sidx, loc.at[0])
+    cp_idx.start()
     cp_up = pltpu.make_async_copy(wup, wraw, loc.at[1])
     cp_dn = pltpu.make_async_copy(wdn, wd, loc.at[2])
     own_rows = pltpu.make_async_copy(uniq.at[me], land.at[me], loc.at[3])
@@ -311,12 +312,28 @@
     cp_up.start()
     cp_dn.start()
     cp_m1.start()
+    wide = C * S
+    fold_s = ((iota((wide, T), 0) & (S - 1)) == (iota((wide, T), 1) & (S - 1))).astype(F32)
+    of_peer = (iota((C, wide), 1) >> 4) == iota((C, wide), 0)
+    cp_idx.wait()
+    listed = sidx[...].astype(F32)
+    spread_d = [
+        jnp.where(of_peer, jnp.broadcast_to(listed[d : d + 1, :], (C, wide)), 0.0) for d in range(D)
+    ]
+    spread_d = matmul(jnp.concatenate(spread_d, 0).astype(BF16), fold_s.astype(BF16))
+    spread_d = spread_d.reshape(D, C, T)
+    packed = jnp.sum(
+        jnp.where((iota((D, C, T), 2) >> 4) == iota((D, C, T), 0), spread_d, 0.0), 0
+    ).astype(jnp.int32)
+    for p in range(C):
+        isend[p] = packed[p : p + 1, :]
+    iland[me] = isend[me]
     pl.semaphore_wait(barrier, C)
 
     order = sorted(range(1, C), key=lambda i: -min(i, C - i))
     for i in order:
         p = to_col(i)
-        rcopy(tile(p), iland.at[me], sa.at[0], ra.at[0], {"col": p}).start()
+        rcopy(isend.at[p], iland.at[me], sa.at[0], ra.at[0], {"col": p}).start()
     for i in order:
         p = to_col(i)
         rcopy(uniq.at[p], land.at[me], sa.at[1], ra.at[1], {"col": p}).start()
@@ -367,12 +384,12 @@
                 target == jnp.broadcast_to(local[d : d + 1, :], (T, T)), 1.0, 0.0
             ).astype(BF16)
 
-    own_idx.wait()
     all_idx.wait_recv()
-    ix = iland[...].astype(F32).reshape(T, T)
-    mine = lax.rem(me, T // S) * S
-    tiled = (iota((T, T), 0) == (iota((T, T), 1) & (S - 1)) + mine).astype(F32)
-    idx_n = matmul(ix, tiled, precision=HIGH)
+    group = (iota((D, T), 1) >> 4) == iota((D, T), 0)
+    ix = [
+        jnp.where(group, jnp.broadcast_to(iland[p].astype(F32), (D, T)), 0.0) for p in range(C)
+    ]
+    idx_n = matmul(jnp.concatenate(ix, 0).astype(BF16), fold_s[0:T].astype(BF16))
     idxn[...] = idx_n
     idx_t = idx_n.T
     for u in range(U):
@@ -693,6 +710,7 @@
         out_specs=(vmem,) * 5,
         scratch_shapes=[
             pltpu.VMEM((D, 8, C), jnp.int32),
+            pltpu.VMEM((D, C * S), jnp.int32),
             pltpu.VMEM((8, T), BF16),
             pltpu.VMEM((1, flat), F32),
             pltpu.VMEM((8, T), BF16),
@@ -700,8 +718,9 @@
             pltpu.VMEM((1, width), F32),
             pltpu.VMEM((S, 16 * width), BF16),
             pltpu.VMEM((S, wide), BF16),
+            pltpu.VMEM((C, 1, T), jnp.int32),
             pltpu.VMEM((C, D, wide), BF16),
-            pltpu.VMEM((C, D, T), jnp.int32),
+            pltpu.VMEM((C, 1, T), jnp.int32),
             pltpu.VMEM((flat, hid), BF16),
             pltpu.VMEM((flat, hid), BF16),
             pltpu.VMEM((hid, wide), BF16),

time: 47.1 us -> 46.1 us (0.979)
  Pallas kernels: 46.3 us -> 45.2 us
    pallas_call x1, Pallas kernels: 45 us -> 43.9 us  [fast_body(): pl.pallas_call(functools.partial(fused_kernel, C, D), out_shape=(pltpu.VM...]
where the time goes in v4:
time: 46.1 us; the launch traced here: 45.9 us
  Pallas kernels  45.2 us (98%)
  between operations  0.64 us (1%)
    pallas_call x1, Pallas kernels, fast_body(): pl.pallas_call(functools.partial(fused_kernel, C, D), out_shape=(pltpu.VM...  43.9 us
    pallas_call x1, Pallas kernels, fast_body(): pl.pallas_call(functools.partial(moment_kernel, width), out_shape=(jax.Sh...  1.32 us

profile of v4, /device:TPU:0, one launch (start us, length us, event | category | flops | bytes accessed | tf_op | source)
XLA Modules:
  0.0 45.9 jit_solution(2459854118921939314)
XLA Ops:
  0.6 43.9 %wukong_step.1 = (bf16[16,3072]{1,0:T(8,128)(2,1)S(1)}, f32[8,192,128]{2,1,0:T(8,128)S(1)}, bf16[8,192,128]{2,1,0:T(8,128)(2,1)S(1)}, f32[8,192,128]{2,1,0:T(8,128)S(1)}, f32[8,128]{1,0:T(8,128)S(1)}) custom-call(bf16[16,8,1536]{2,1,0:T(8,128)(2,1)} %uniq.1, s32[8,8,16]{2,1,0:T(8,128)} %bitcast.9, s32[8,256]{1,0:T(8,128)} %bitcast.10, ...), custom_call_target="tpu_custom_call" | custom-call | tf_op jit(solution)/shard_map/wukong_step/pallas_call | solution.py:700
  44.5 1.3 %moments.1 = (bf16[16,3072]{1,0:T(8,128)(2,1)}, f32[8,192,128]{2,1,0:T(8,128)}, f32[8,128]{1,0:T(8,128)}, f32[8,192,128]{2,1,0:T(8,128)}) custom-call(bf16[16,3072]{1,0:T(8,128)(2,1)S(1)} %get-tuple-element.13.lay, f32[8,192,128]{2,1,0:T(8,128)S(1)} %get-tuple-element.14.own, bf16[8,192,128]{2,1,0:T(8,128)(2,1)S(1)} %get-tuple-element.15.got, ...), custom_call_target="tpu_custom_call" | custom-call | tf_op jit(solution)/shard_map/moments/pallas_call | solution.py:790

commit v5 on v4

--- a/solution.py
+++ b/solution.py
@@ -259,8 +259,10 @@
     mr = lax.axis_index("row")
     other = 1 - mr
 
+    bits = [1 - 2 * lax.rem(me // (1 << b), 2) for b in range(4)]
+
     def to_col(i):
-        return lax.rem(me + i, C)
+        return me + sum(bits[b] * (1 << b) for b in range(4) if i >> b & 1)
 
     def rcopy(src, dst, ssem, rsem, where):
         return pltpu.make_async_remote_copy(
@@ -330,7 +332,7 @@
     iland[me] = isend[me]
     pl.semaphore_wait(barrier, C)
 
-    order = sorted(range(1, C), key=lambda i: -min(i, C - i))
+    order = range(C - 1, 0, -1)
     for i in order:
         p = to_col(i)
         rcopy(isend.at[p], iland.at[me], sa.at[0], ra.at[0], {"col": p}).start()

time: 46.1 us -> 45 us (0.976)
  Pallas kernels: 45.2 us -> 44.2 us
    pallas_call x1, Pallas kernels: 43.9 us -> 42.8 us  [fast_body(): pl.pallas_call(functools.partial(fused_kernel, C, D), out_shape=(pltpu.VM...]
where the time goes in v5:
time: 45 us; the launch traced here: 44.8 us
  Pallas kernels  44.2 us (98%)
  between operations  0.64 us (1%)
    pallas_call x1, Pallas kernels, fast_body(): pl.pallas_call(functools.partial(fused_kernel, C, D), out_shape=(pltpu.VM...  42.8 us
    pallas_call x1, Pallas kernels, fast_body(): pl.pallas_call(functools.partial(moment_kernel, width), out_shape=(jax.Sh...  1.32 us

profile of v5, /device:TPU:0, one launch (start us, length us, event | category | flops | bytes accessed | tf_op | source)
XLA Modules:
  0.0 44.8 jit_solution(13712466161635245299)
XLA Ops:
  0.6 42.8 %wukong_step.1 = (bf16[16,3072]{1,0:T(8,128)(2,1)S(1)}, f32[8,192,128]{2,1,0:T(8,128)S(1)}, bf16[8,192,128]{2,1,0:T(8,128)(2,1)S(1)}, f32[8,192,128]{2,1,0:T(8,128)S(1)}, f32[8,128]{1,0:T(8,128)S(1)}) custom-call(bf16[16,8,1536]{2,1,0:T(8,128)(2,1)} %uniq.1, s32[8,8,16]{2,1,0:T(8,128)} %bitcast.9, s32[8,256]{1,0:T(8,128)} %bitcast.10, ...), custom_call_target="tpu_custom_call" | custom-call | tf_op jit(solution)/shard_map/wukong_step/pallas_call | solution.py:702
  43.5 1.3 %moments.1 = (bf16[16,3072]{1,0:T(8,128)(2,1)}, f32[8,192,128]{2,1,0:T(8,128)}, f32[8,128]{1,0:T(8,128)}, f32[8,192,128]{2,1,0:T(8,128)}) custom-call(bf16[16,3072]{1,0:T(8,128)(2,1)S(1)} %get-tuple-element.13.lay, f32[8,192,128]{2,1,0:T(8,128)S(1)} %get-tuple-element.14.own, bf16[8,192,128]{2,1,0:T(8,128)(2,1)S(1)} %get-tuple-element.15.got, ...), custom_call_target="tpu_custom_call" | custom-call | tf_op jit(solution)/shard_map/moments/pallas_call | solution.py:792
